TPU v7x, 256 devices: a whole 4x4x8 slice. The times are simulated.
256 devices in a mesh: dp: 16 (over z, core), expert: 16 (over y, x).
Axes of the slice: x: 4, y: 4, z: 8, core: 2. Of those that a mesh axis runs over, the one named last changes fastest.
Arguments:
- cotangent: bfloat16 [32768, 2048], P(('dp', 'expert')), may hold values from -6 to 6
- saved_gate_up: bfloat16 [32768, 8, 1536], P(('dp', 'expert')), may hold values from -6 to 6
- route_ids: int32 [32768, 8], P(('dp', 'expert')), may hold values from 0 to 31, all different within a row; in each aligned block of 128 rows (0 to 127, 128 to 255, ...) at most 64 rows name the same one
- route_weights: float32 [32768, 8], P(('dp', 'expert')), may hold values from 0.05 to 1
- w_down: bfloat16 [32, 768, 2048], P('expert', 'dp'), may hold values from -0.21875 to 0.21875
Outputs:
- grad_gate_up: bfloat16 [32768, 8, 1536], P(('dp', 'expert'))
- route_grad: float32 [32768, 8], P(('dp', 'expert'))
- grad_down: float32 [32, 768, 2048], P('expert', 'dp')
Inputs may be any that keep to these rules, and one draw needn't show every extreme that they name: `route_ids`: within the rows of one device (aligned blocks of 128 tokens), no expert is named by more than 64 routes, and in every draw some expert is named by exactly 64; the 8 experts of a token are distinct.
All inputs are finite; a program needn't handle non-finite values.
Results may differ from a plain program's by a relative error of at most 0.02.
Values may be sent and summed in bfloat16 or wider, within the bound.
A program may use at most 128 MiB of HBM per device.

v0:
```python
import jax
import jax.numpy as jnp
from jax import lax
from jax.sharding import PartitionSpec as P


def slot_counts(ids, experts):
    routes = ids.shape[-1]
    onehot = (ids[..., None] == jnp.arange(experts, dtype=jnp.int32)).astype(jnp.bfloat16)
    lower = (jnp.arange(routes)[:, None] > jnp.arange(routes)[None, :]).astype(jnp.bfloat16)
    before = jnp.einsum("rq,...qe->...re", lower, onehot, preferred_element_type=jnp.float32)
    return jnp.sum(before * onehot.astype(jnp.float32), axis=-1).astype(jnp.int32)


def local(cotangent, saved_gate_up, route_ids, route_weights, w_down):
    tokens, top = route_ids.shape
    width = cotangent.shape[1]
    hidden_units = saved_gate_up.shape[2] // 2
    owners = lax.axis_size("expert")
    replicas = lax.axis_size("dp")
    me = lax.axis_index("expert")
    local_experts = w_down.shape[0]
    experts = local_experts * owners
    capacity = min(tokens, 2 * tokens * top // experts)
    routes = tokens * top
    cot_group = lax.all_gather(cotangent, "expert", axis=0, tiled=True)
    ids_group = lax.all_gather(route_ids.reshape(1, routes), "expert", axis=0, tiled=True)
    full_down = lax.all_gather(w_down, "dp", axis=1, tiled=True)
    gate = saved_gate_up[:, :, :hidden_units].astype(jnp.float32)
    up = saved_gate_up[:, :, hidden_units:].astype(jnp.float32)
    sig = jax.nn.sigmoid(gate)
    act = gate * sig
    hidden = (act * up).astype(jnp.bfloat16)
    weights = route_weights[:, :, None]
    scaled = (weights * hidden.astype(jnp.float32)).astype(jnp.bfloat16)
    flat_ids = route_ids.reshape(routes)
    slot = slot_counts(flat_ids, experts)
    position = flat_ids * capacity + slot
    slot_ids = jnp.arange(experts * capacity, dtype=jnp.int32)
    match = position[None, :] == slot_ids[:, None]
    route_of_slot = jnp.sum(
        jnp.where(match, jnp.arange(routes, dtype=jnp.int32)[None, :], 0), axis=1
    )
    filled = jnp.any(match, axis=1)
    h_rows = jnp.where(
        filled[:, None],
        scaled.reshape(routes, hidden_units)[route_of_slot],
        jnp.zeros((), jnp.bfloat16),
    )
    h_send = h_rows.reshape(owners, local_experts, capacity, hidden_units)
    slot_all = slot_counts(ids_group, experts)
    mine = me * local_experts + jnp.arange(local_experts, dtype=jnp.int32)
    pos_all = ids_group * capacity + slot_all
    want = (mine[:, None] * capacity + jnp.arange(capacity, dtype=jnp.int32)[None, :]).reshape(-1)
    hit = pos_all[:, None, :] == want[None, :, None]
    token_of = jnp.sum(
        jnp.where(hit, (jnp.arange(routes, dtype=jnp.int32) // top)[None, None, :], 0), axis=2
    )
    rows = (jnp.arange(owners, dtype=jnp.int32)[:, None] * tokens + token_of).reshape(
        owners, local_experts, capacity
    )
    rows = jnp.transpose(rows, (1, 0, 2)).reshape(local_experts, owners * capacity)
    h_recv = lax.all_to_all(h_send, "expert", split_axis=0, concat_axis=2, tiled=True)[0]
    h_recv, cot_group = lax.optimization_barrier((h_recv, cot_group))
    dy_recv = cot_group[rows]
    grads = jnp.einsum(
        "jsd,jfd->jsf", dy_recv, full_down, preferred_element_type=jnp.float32
    ).astype(jnp.bfloat16)
    back = lax.all_to_all(
        grads.reshape(1, local_experts, owners * capacity, hidden_units),
        "expert",
        split_axis=2,
        concat_axis=0,
        tiled=True,
    )
    parts = []
    for j in range(local_experts):
        part = jnp.einsum(
            "sf,sd->fd", h_recv[j], dy_recv[j], preferred_element_type=jnp.float32
        ).astype(jnp.bfloat16)
        parts.append(part.reshape(replicas, hidden_units // replicas, width))
    summed = lax.psum_scatter(jnp.stack(parts, axis=1), "dp", scatter_dimension=0, tiled=True)
    grad_down = summed[0].astype(jnp.float32)
    returned_rows = back.reshape(experts * capacity, hidden_units)[position]
    qf = returned_rows.reshape(tokens, top, hidden_units).astype(jnp.float32)
    route_grad = jnp.sum(qf * hidden.astype(jnp.float32), -1)
    d_hidden = weights * qf
    d_gate = d_hidden * up * sig * (1.0 + gate * (1.0 - sig))
    d_up = d_hidden * act
    grad_gate_up = jnp.concatenate([d_gate, d_up], -1).astype(jnp.bfloat16)
    return (grad_gate_up, route_grad, grad_down)


def solution(mesh):
    return jax.shard_map(
        local,
        mesh=mesh,
        in_specs=(
            P(("dp", "expert"), None),
            P(("dp", "expert"), None, None),
            P(("dp", "expert"), None),
            P(("dp", "expert"), None),
            P("expert", "dp", None),
        ),
        out_specs=(
            P(("dp", "expert"), None, None),
            P(("dp", "expert"), None),
            P("expert", "dp", None),
        ),
        check_vma=False,
    )
```

profile of v0, /device:TPU:1, one launch (start us, length us, event | category | flops | bytes accessed | tf_op | source)
XLA Modules:
  0.0 258.9 jit_solution(17816790262172470901)
XLA Ops:
  7.2 0.0 all-gather.4.cloned.1.call-start
  7.2 0.7 all-gather.4.cloned.1.call-update
  7.9 0.0 all-gather.6.cloned.1.call-start
  7.9 0.7 all-gather.6.cloned.1.call-update
  8.6 0.8 copy.43
  9.4 0.1 reshape.170
  9.5 0.8 copy.42
  10.3 0.5 fusion.35
  10.9 1.0 fusion
  11.9 0.1 broadcast_in_dim.34
  12.0 0.9 select_reduce_fusion.1
  12.9 3.4 %fusion.29 = (bf16[1024,768]{1,0:T(8,128)(2,1)S(1)}, bf16[128,8,768]{2,1,0:T(8,128)(2,1)}) fusion(f32[128,8]{1,0:T(8,128)S(1)} %copy.42, bf16[128,8,1536]{2,1,0:T(8,128)(2,1)} %param.6), kind=kLoop, calls=%fused_computation.45 | loop fusion | flops 8650752 | bytes 6295552 | tf_op jit(solution)/shard_map/reshape | solution.py:47
  16.3 9.4 %gather_fusion = bf16[2048,768]{1,0:T(8,128)(2,1)} fusion(bf16[1024,768]{1,0:T(8,128)(2,1)S(1)} %get-tuple-element.13, s32[2048]{0:T(1024)S(1)} %broadcast_clamp_fusion), kind=kCustom, calls=%fused_computation | custom fusion | bytes 6299648 | tf_op jit(solution)/shard_map/gather | solution.py:47
  25.7 3.5 %broadcast_select_fusion = bf16[16,2,64,768]{3,2,1,0:T(8,128)(2,1)} fusion(bf16[16,2,64,768]{3,2,1,0:T(8,128)(2,1)} %bitcast.64, pred[16,2,64]{2,1,0:T(4,128)(4,1)S(1)} %broadcast_in_dim.34), kind=kLoop, calls=%fused_computation.40 | loop fusion | flops 1572864 | bytes 6293504 | tf_op jit(solution)/shard_map/jit(_where)/select_n | solution.py:45
  29.2 7.5 %all-to-all-start = ((bf16[16,2,64,768]{3,2,1,0:T(8,128)(2,1)}), bf16[16,2,64,768]{3,2,1,0:T(8,128)(2,1)S(1)}, u32[]{:S(2)}, u32[]{:S(2)}) async-start(bf16[16,2,64,768]{3,2,1,0:T(8,128)(2,1)} %broadcast_select_fusion), calls=%async_computation | async-start | bytes 6291456 | tf_op jit(solution)/shard_map/all_to_all | solution.py:63
  36.7 0.0 reduce-scatter.2.cloned.1.call-start
  36.8 0.1 reshape.207
  36.9 69.4 %all-gather = s32[16,1,1024]{2,1,0:T(1,128)S(1)} all-gather(s32[1,1,1024]{2,1,0:T(1,128)S(1)} %reshape.207), channel_id=1, replica_groups=mesh['dp'=16,'expert'=16] {'expert'}, dimensions={0}, use_global_device_ids=true | all-gather | bytes 69632 | tf_op jit(solution)/shard_map/all_gather | solution.py:27
  106.3 0.1 iota_add_fusion
  106.4 0.1 add.121
  106.4 1.4 fusion.27
  107.9 1.0 select_reduce_fusion
  108.9 0.1 reduce_sum.54
  109.0 0.1 add_bitcast_fusion
  109.1 0.1 reshape.173
  109.2 0.0 all-to-all-done
  109.2 1.9 copy.44
  111.0 6.2 %all-gather.4.cloned.1.call-done = bf16[2048,2048]{1,0:T(8,128)(2,1)} async-done(((bf16[128,2048]{1,0:T(8,128)(2,1)}), bf16[2048,2048]{1,0:T(8,128)(2,1)}) %all-gather.4.cloned.1.call-update) | async-done | bytes 8388624 | tf_op jit(solution)/shard_map/all_gather | solution.py:26
  117.3 21.1 %gather_fusion.1 = bf16[2048,2048]{1,0:T(8,128)(2,1)} fusion(bf16[2048,2048]{1,0:T(8,128)(2,1)} %all-gather.4.cloned.1.call-done, s32[2048]{0:T(1024)S(1)} %bitcast_clamp_fusion), kind=kCustom, calls=%fused_computation.1 | custom fusion | bytes 16785408 | tf_op jit(solution)/shard_map/gather | solution.py:65
  138.4 0.0 copy-done.2
  138.4 6.1 %fusion.10 = bf16[768,2048]{1,0:T(8,128)(2,1)S(1)} fusion(bf16[2048,2048]{1,0:T(8,128)(2,1)} %gather_fusion.1, bf16[2,1024,768]{2,1,0:T(8,128)(2,1)S(1)} %bitcast.66), kind=kOutput, calls=%fused_computation.25 | convolution fusion | flops 3222798336 | bytes 8912896 | tf_op jit(solution)/shard_map/sf,sd->fd/dot_general | solution.py:78
  144.5 3.7 %fusion.13 = bf16[768,2048]{1,0:T(8,128)(2,1)S(1)} fusion(bf16[2048,2048]{1,0:T(8,128)(2,1)S(1)} %copy-done.1, bf16[2,1024,768]{2,1,0:T(8,128)(2,1)S(1)} %bitcast.67), kind=kOutput, calls=%fused_computation.26 | convolution fusion | flops 3222798336 | bytes 8912896 | tf_op jit(solution)/shard_map/sf,sd->fd/dot_general | solution.py:78
  148.2 3.3 %pad_maximum_fusion = bf16[16,2,48,2048]{3,2,1,0:T(8,128)(2,1)} fusion(bf16[16,1,48,2048]{3,2,1,0:T(8,128)(2,1)S(1)} %bitcast.69, bf16[16,1,48,2048]{3,2,1,0:T(8,128)(2,1)S(1)} %bitcast.68), kind=kLoop, calls=%fused_computation.7 | loop fusion | flops 3145728 | bytes 12582912 | tf_op jit(solution)/shard_map/stack | solution.py:82
  151.5 0.0 reduce-scatter.2.cloned.1.call-update
  151.5 12.3 %all-gather.6.cloned.1.call-done = bf16[2,768,2048]{2,1,0:T(8,128)(2,1)} async-done(((bf16[2,48,2048]{2,1,0:T(8,128)(2,1)}), bf16[2,768,2048]{2,1,0:T(8,128)(2,1)}) %all-gather.6.cloned.1.call-update) | async-done | bytes 6291472 | tf_op jit(solution)/shard_map/all_gather | solution.py:28
  163.8 11.0 %convert_bitcast_fusion = bf16[1,2,1024,768]{3,2,1,0:T(8,128)(2,1)S(1)} fusion(bf16[2,1024,2048]{2,1,0:T(8,128)(2,1)} %bitcast.65, bf16[2,768,2048]{2,1,0:T(8,128)(2,1)} %all-gather.6.cloned.1.call-done), kind=kOutput, calls=%fused_computation.39 | convolution fusion | flops 6444023808 | bytes 17825792 | tf_op jit(solution)/shard_map/jsd,jfd->jsf/dot_general | solution.py:66
  174.8 4.9 %copy.47 = bf16[1,2,1024,768]{3,1,0,2:T(2,128)(2,1)} copy(bf16[1,2,1024,768]{3,2,1,0:T(8,128)(2,1)S(1)} %convert_bitcast_fusion) | data formatting | bytes 6291456 | tf_op jit(solution)/shard_map/reshape | solution.py:70
  179.7 6.7 %all-to-all-start.1 = ((bf16[1,2,1024,768]{3,1,0,2:T(2,128)(2,1)}), bf16[1,2,1024,768]{3,1,0,2:T(2,128)(2,1)S(1)}, u32[]{:S(2)}, u32[]{:S(2)}) async-start(bf16[1,2,1024,768]{3,1,0,2:T(2,128)(2,1)} %copy.47), calls=%async_computation.1 | async-start | bytes 6291456 | tf_op jit(solution)/shard_map/all_to_all | solution.py:69
  186.4 0.1 copy.49
  186.5 0.1 mul.108
  186.6 47.5 %all-to-all-done.1 = bf16[1,2,1024,768]{3,1,0,2:T(2,128)(2,1)S(1)} async-done(((bf16[1,2,1024,768]{3,1,0,2:T(2,128)(2,1)}), bf16[1,2,1024,768]{3,1,0,2:T(2,128)(2,1)S(1)}, u32[]{:S(2)}, u32[]{:S(2)}) %all-to-all-start.1) | async-done | bytes 3145760 | tf_op jit(solution)/shard_map/all_to_all | solution.py:69
  234.2 1.7 copy-done
  235.9 2.5 copy.48
  238.4 5.2 %gather_fusion.2 = bf16[1024,768]{1,0:T(8,128)(2,1)} fusion(bf16[2048,768]{1,0:T(8,128)(2,1)S(1)} %bitcast.62, s32[1024]{0:T(1024)S(1)} %broadcast_clamp_fusion.1), kind=kCustom, calls=%fused_computation.2 | custom fusion | bytes 3149824 | tf_op jit(solution)/shard_map/gather | solution.py:84
  243.6 4.2 %fusion.20 = (bf16[128,8,768]{2,1,0:T(8,128)(2,1)S(1)}, bf16[128,8,768]{2,1,0:T(8,128)(2,1)S(1)}, f32[128,8]{1,0:T(8,128)S(1)}) fusion(bf16[1024,768]{1,0:T(8,128)(2,1)} %gather_fusion.2, f32[128,8]{1,0:T(8,128)S(1)} %copy.42, bf16[128,8,1536]{2,1,0:T(8,128)(2,1)} %param.6, bf16[128,8,768]{2,1,0:T(8,128)(2,1)} %get-tuple-element.14), kind=kLoop, calls=%fused_computation.31 | loop fusion | flops 15727616 | bytes 9445376 | tf_op jit(solution)/shard_map/convert.2
  247.8 0.7 copy.52
  248.5 1.9 pad_maximum_fusion.1
  250.4 1.9 bitcast_convert_fusion
  (22 shorter events, 0.1 us)
Async XLA Ops:
  7.2 110.1 %all-gather.4.cloned.1.call-start = ((), (), s32[]{:S(2)}) async-start(), calls=%async_computation.3 | async-start | bytes 8912896 | tf_op jit(solution)/shard_map/all_gather | solution.py:26
  7.9 155.9 %all-gather.6.cloned.1.call-start = ((), (), s32[]{:S(2)}) async-start(), calls=%async_computation.4 | async-start | bytes 6684672 | tf_op jit(solution)/shard_map/all_gather | solution.py:28
  29.2 80.0 %all-to-all-start = ((bf16[16,2,64,768]{3,2,1,0:T(8,128)(2,1)}), bf16[16,2,64,768]{3,2,1,0:T(8,128)(2,1)S(1)}, u32[]{:S(2)}, u32[]{:S(2)}) async-start(bf16[16,2,64,768]{3,2,1,0:T(8,128)(2,1)} %broadcast_select_fusion), calls=%async_computation | async-start | bytes 6291456 | tf_op jit(solution)/shard_map/all_to_all | solution.py:63
  36.7 213.7 %reduce-scatter.2.cloned.1.call-start = ((), (), s32[]{:S(2)}) async-start(), calls=%async_computation.5 | async-start | bytes 6684672 | tf_op jit(solution)/shard_map/reduce_scatter | solution.py:82
  117.3 21.1 %copy-start.2 = (bf16[16,2,64,768]{3,2,0,1:T(8,128)(2,1)S(1)}, bf16[16,2,64,768]{3,2,0,1:T(8,128)(2,1)}, u32[]{:S(2)}) copy-start(bf16[16,2,64,768]{3,2,0,1:T(8,128)(2,1)} %copy.44) | copy-start | bytes 9437188
  138.4 6.1 %copy-start.1 = (bf16[2048,2048]{1,0:T(8,128)(2,1)S(1)}, bf16[2048,2048]{1,0:T(8,128)(2,1)}, u32[]{:S(2)}) copy-start(bf16[2048,2048]{1,0:T(8,128)(2,1)} %gather_fusion.1) | copy-start | bytes 25165828
  179.7 6.7 %copy-start.3 = (s32[128,8]{0,1:T(8,128)S(1)}, s32[128,8]{0,1:T(8,128)}, u32[]{:S(2)}) copy-start(s32[128,8]{0,1:T(8,128)} %param.7) | copy-start | bytes 12292
  179.7 54.5 %all-to-all-start.1 = ((bf16[1,2,1024,768]{3,1,0,2:T(2,128)(2,1)}), bf16[1,2,1024,768]{3,1,0,2:T(2,128)(2,1)S(1)}, u32[]{:S(2)}, u32[]{:S(2)}) async-start(bf16[1,2,1024,768]{3,1,0,2:T(2,128)(2,1)} %copy.47), calls=%async_computation.1 | async-start | bytes 6291456 | tf_op jit(solution)/shard_map/all_to_all | solution.py:69
  234.2 1.7 copy-start
Sparse Core Ops, SparseCore 0:
  10.4 106.7 all-gather.3
  119.1 44.6 all-gather.5
  166.4 62.4 reduce-scatter.1
where the time goes:
time: 259 us
  blocking collectives  69.4 us (27%)
  waiting for transfers between devices  67.4 us (26%)
  local copies, waits for them, and re-layouts  49.7 us (19%)
  matrix products  22.8 us (9%)
  other arithmetic  21.4 us (8%)
  starting transfers between devices  14.3 us (6%)
  between operations  14 us (5%)
    all_gather x1, blocking collectives, local(): lax.all_gather(route_ids.reshape(1, routes), 'expert', axis=0, tiled=True)  69.4 us
    all_to_all x1, waiting for transfers between devices, local(): lax.all_to_all(grads.reshape(1, local_experts, owners * capacity, hidden_...  47.5 us
    gather x1, local copies, waits for them, and re-layouts, local(): dy_recv = cot_group[rows]  21.1 us
    all_gather x1, waiting for transfers between devices, local(): full_down = lax.all_gather(w_down, 'dp', axis=1, tiled=True)  12.3 us
    dot_general x1, matrix products, local(): jnp.einsum('jsd,jfd->jsf', dy_recv, full_down, preferred_element_type=jnp...  11 us
    dot_general x2, matrix products, local(): jnp.einsum('sf,sd->fd', h_recv[j], dy_recv[j], preferred_element_type=jnp...  9.8 us
    gather x1, local copies, waits for them, and re-layouts, local(): scaled.reshape(routes, hidden_units)[route_of_slot]  9.4 us
    all_to_all x1, starting transfers between devices, local(): lax.all_to_all(h_send, 'expert', split_axis=0, concat_axis=2, tiled=True)[0]  7.51 us
  transfers between devices with their start and end apart: 5, of which 3 were waited for; matrix products, arithmetic and copies ran while one was open for 35% of the time, Pallas kernels for 0%

commit v1 on v0

--- a/solution.py
+++ b/solution.py
@@ -25,7 +25,9 @@
     routes = tokens * top
     cot_group = lax.all_gather(cotangent, "expert", axis=0, tiled=True)
     ids_group = lax.all_gather(route_ids.reshape(1, routes), "expert", axis=0, tiled=True)
-    full_down = lax.all_gather(w_down, "dp", axis=1, tiled=True)
+    full_down = jnp.concatenate(
+        lax.all_to_all(jnp.stack([w_down] * lax.axis_size("dp")), "dp", 0, 0), axis=1
+    )
     gate = saved_gate_up[:, :, :hidden_units].astype(jnp.float32)
     up = saved_gate_up[:, :, hidden_units:].astype(jnp.float32)
     sig = jax.nn.sigmoid(gate)

time: 259 us -> 336 us (1.30)
  waiting for transfers between devices: 67.4 us -> 143 us
  local copies, waits for them, and re-layouts: 49.7 us -> 56.6 us
    all_to_all x1, waiting for transfers between devices: 0.01 us -> 93.8 us  [local(): lax.all_to_all(jnp.stack([w_down] * lax.axis_size('dp')), 'dp', 0, 0)]
    all_gather x1, blocking collectives: 69.4 us -> 18.9 us  [local(): lax.all_gather(route_ids.reshape(1, routes), 'expert', axis=0, tiled=True)]
    all_to_all x0 -> x1, blocking collectives: none -> 48.9 us  [local(): lax.all_to_all(h_send, 'expert', split_axis=0, concat_axis=2, tiled=True)[0]]
    all_gather x1 -> x0, waiting for transfers between devices: 12.3 us -> none  [local(): full_down = lax.all_gather(w_down, 'dp', axis=1, tiled=True)]
    all_gather x1, waiting for transfers between devices: 6.22 us -> 0.01 us  [local(): cot_group = lax.all_gather(cotangent, 'expert', axis=0, tiled=True)]
    reshape x0 -> x1, local copies, waits for them, and re-layouts: none -> 3.48 us  [local(): jnp.concatenate(lax.all_to_all(jnp.stack([w_down] * lax.axis_size('dp')),...]
    another operation x0 -> x1, local copies, waits for them, and re-layouts: none -> 3.45 us  [local(): jnp.stack([w_down] * lax.axis_size('dp'))]
  transfers between devices with their start and end apart: 5 -> 4, of which waited for: 3 -> 2; matrix products, arithmetic and copies ran while one was open for 35% -> 28% of each run, Pallas kernels for 0% -> 0%
where the time goes in v1:
time: 336 us
  waiting for transfers between devices  143 us (43%)
  blocking collectives  67.8 us (20%)
  local copies, waits for them, and re-layouts  56.6 us (17%)
  matrix products  20.9 us (6%)
  other arithmetic  20.2 us (6%)
  between operations  14.3 us (4%)
  starting transfers between devices  12.9 us (4%)
    all_to_all x1, waiting for transfers between devices, local(): lax.all_to_all(jnp.stack([w_down] * lax.axis_size('dp')), 'dp', 0, 0)  93.8 us
    all_to_all x1, blocking collectives, local(): lax.all_to_all(h_send, 'expert', split_axis=0, concat_axis=2, tiled=True)[0]  48.9 us
    all_to_all x1, waiting for transfers between devices, local(): lax.all_to_all(grads.reshape(1, local_experts, owners * capacity, hidden_...  48.9 us
    gather x1, local copies, waits for them, and re-layouts, local(): dy_recv = cot_group[rows]  21.1 us
    all_gather x1, blocking collectives, local(): lax.all_gather(route_ids.reshape(1, routes), 'expert', axis=0, tiled=True)  18.9 us
    dot_general x2, matrix products, local(): jnp.einsum('sf,sd->fd', h_recv[j], dy_recv[j], preferred_element_type=jnp...  9.73 us
    gather x1, local copies, waits for them, and re-layouts, local(): scaled.reshape(routes, hidden_units)[route_of_slot]  9.4 us
    dot_general x1, matrix products, local(): jnp.einsum('jsd,jfd->jsf', dy_recv, full_down, preferred_element_type=jnp...  9.19 us
  transfers between devices with their start and end apart: 4, of which 2 were waited for; matrix products, arithmetic and copies ran while one was open for 28% of the time, Pallas kernels for 0%

profile of v1, /device:TPU:1, one launch (start us, length us, event | category | flops | bytes accessed | tf_op | source)
XLA Modules:
  0.0 336.0 jit_solution(13003331292949876427)
XLA Ops:
  7.2 0.0 all-gather.3.cloned.1.call-start
  7.2 0.7 all-gather.3.cloned.1.call-update
  7.9 0.8 copy.43
  8.7 0.8 copy.44
  9.5 0.1 reshape.178
  9.6 0.5 fusion.35
  10.1 1.0 fusion
  11.2 0.1 broadcast_in_dim.34
  11.2 0.9 select_reduce_fusion.1
  12.2 3.4 %fusion.29 = (bf16[1024,768]{1,0:T(8,128)(2,1)S(1)}, bf16[128,8,768]{2,1,0:T(8,128)(2,1)}) fusion(f32[128,8]{1,0:T(8,128)S(1)} %copy.43, bf16[128,8,1536]{2,1,0:T(8,128)(2,1)} %param.6), kind=kLoop, calls=%fused_computation.45 | loop fusion | flops 8650752 | bytes 6295552 | tf_op jit(solution)/shard_map/reshape | solution.py:49
  15.6 9.4 %gather_fusion = bf16[2048,768]{1,0:T(8,128)(2,1)} fusion(bf16[1024,768]{1,0:T(8,128)(2,1)S(1)} %get-tuple-element.13, s32[2048]{0:T(1024)S(1)} %broadcast_clamp_fusion), kind=kCustom, calls=%fused_computation | custom fusion | bytes 6299648 | tf_op jit(solution)/shard_map/gather | solution.py:49
  25.0 2.3 broadcast_select_fusion
  27.2 0.0 copy-start.3
  27.2 48.9 %all_to_all.35 = bf16[16,2,64,768]{3,2,1,0:T(8,128)(2,1)S(1)} all-to-all(bf16[16,2,64,768]{3,2,1,0:T(8,128)(2,1)S(1)} %broadcast_select_fusion), channel_id=1, replica_groups=mesh['dp'=16,'expert'=16] {'expert'}, dimensions={0} | all-to-all | bytes 6291456 | tf_op jit(solution)/shard_map/all_to_all | solution.py:65
  76.2 0.0 copy-done.3
  76.2 3.4 %stack.4 = bf16[16,2,48,2048]{3,2,1,0:T(8,128)(2,1)} broadcast(bf16[2,48,2048]{2,1,0:T(8,128)(2,1)S(1)} %copy-done.3), dimensions={1,2,3} | broadcast | bytes 6684672 | tf_op jit(solution)/shard_map/stack | solution.py:29
  79.6 8.8 %all-to-all-start.1 = ((bf16[16,2,48,2048]{3,2,1,0:T(8,128)(2,1)}), bf16[16,2,48,2048]{3,2,1,0:T(8,128)(2,1)}, u32[]{:S(2)}, u32[]{:S(2)}) async-start(bf16[16,2,48,2048]{3,2,1,0:T(8,128)(2,1)} %stack.4), calls=%async_computation.1 | async-start | bytes 12582912 | tf_op jit(solution)/shard_map/all_to_all | solution.py:29
  88.4 0.0 reduce-scatter.2.cloned.1.call-start
  88.4 0.1 reshape.217
  88.5 0.1 iota_add_fusion
  88.6 0.1 add.121
  88.7 18.9 %all-gather = s32[16,1,1024]{2,1,0:T(1,128)S(1)} all-gather(s32[1,1,1024]{2,1,0:T(1,128)S(1)} %reshape.217), channel_id=1, replica_groups=mesh['dp'=16,'expert'=16] {'expert'}, dimensions={0}, use_global_device_ids=true | all-gather | bytes 69632 | tf_op jit(solution)/shard_map/all_gather | solution.py:27
  107.6 1.4 fusion.27
  109.1 1.0 select_reduce_fusion
  110.0 0.1 reduce_sum.54
  110.1 0.1 add_bitcast_fusion
  110.2 0.1 reshape.181
  110.3 1.9 copy.45
  112.2 21.1 %gather_fusion.1 = bf16[2048,2048]{1,0:T(8,128)(2,1)} fusion(bf16[2048,2048]{1,0:T(8,128)(2,1)} %all-gather.3.cloned.1.call-done, s32[2048]{0:T(1024)S(1)} %bitcast_clamp_fusion), kind=kCustom, calls=%fused_computation.1 | custom fusion | bytes 16785408 | tf_op jit(solution)/shard_map/gather | solution.py:67
  133.3 6.0 %fusion.13 = bf16[768,2048]{1,0:T(8,128)(2,1)S(1)} fusion(bf16[2048,2048]{1,0:T(8,128)(2,1)} %gather_fusion.1, bf16[2,1024,768]{2,1,0:T(8,128)(2,1)S(1)} %bitcast.69), kind=kOutput, calls=%fused_computation.26 | convolution fusion | flops 3222798336 | bytes 8912896 | tf_op jit(solution)/shard_map/sf,sd->fd/dot_general | solution.py:80
  139.4 3.7 %fusion.10 = bf16[768,2048]{1,0:T(8,128)(2,1)S(1)} fusion(bf16[2048,2048]{1,0:T(8,128)(2,1)S(1)} %copy-done.1, bf16[2,1024,768]{2,1,0:T(8,128)(2,1)S(1)} %bitcast.70), kind=kOutput, calls=%fused_computation.25 | convolution fusion | flops 3222798336 | bytes 8912896 | tf_op jit(solution)/shard_map/sf,sd->fd/dot_general | solution.py:80
  143.1 3.3 pad_maximum_fusion
  146.4 0.0 reduce-scatter.2.cloned.1.call-update
  146.4 93.8 %all-to-all-done.1 = bf16[16,2,48,2048]{3,2,1,0:T(8,128)(2,1)} async-done(((bf16[16,2,48,2048]{3,2,1,0:T(8,128)(2,1)}), bf16[16,2,48,2048]{3,2,1,0:T(8,128)(2,1)}, u32[]{:S(2)}, u32[]{:S(2)}) %all-to-all-start.1) | async-done | bytes 6291488 | tf_op jit(solution)/shard_map/all_to_all | solution.py:29
  240.2 3.5 %copy.48 = bf16[2,16,48,2048]{3,2,1,0:T(8,128)(2,1)S(1)} copy(bf16[2,16,48,2048]{3,2,0,1:T(8,128)(2,1)} %bitcast.11) | data formatting | bytes 12582912 | tf_op jit(solution)/shard_map/reshape | solution.py:28
  243.6 9.2 %convert_bitcast_fusion = bf16[1,2,1024,768]{3,2,1,0:T(8,128)(2,1)S(1)} fusion(bf16[2,1024,2048]{2,1,0:T(8,128)(2,1)} %bitcast.67, bf16[2,768,2048]{2,1,0:T(8,128)(2,1)S(1)} %bitcast.68), kind=kOutput, calls=%fused_computation.39 | convolution fusion | flops 6444023808 | bytes 17825792 | tf_op jit(solution)/shard_map/jsd,jfd->jsf/dot_general | solution.py:68
  252.8 4.9 %copy.49 = bf16[1,2,1024,768]{3,1,0,2:T(2,128)(2,1)} copy(bf16[1,2,1024,768]{3,2,1,0:T(8,128)(2,1)S(1)} %convert_bitcast_fusion) | data formatting | bytes 6291456 | tf_op jit(solution)/shard_map/reshape | solution.py:72
  257.7 4.1 %all-to-all-start.2 = ((bf16[1,2,1024,768]{3,1,0,2:T(2,128)(2,1)}), bf16[1,2,1024,768]{3,1,0,2:T(2,128)(2,1)S(1)}, u32[]{:S(2)}, u32[]{:S(2)}) async-start(bf16[1,2,1024,768]{3,1,0,2:T(2,128)(2,1)} %copy.49), calls=%async_computation.2 | async-start | bytes 6291456 | tf_op jit(solution)/shard_map/all_to_all | solution.py:71
  261.9 0.1 copy.51
  262.0 0.1 mul.108
  262.1 48.9 %all-to-all-done.2 = bf16[1,2,1024,768]{3,1,0,2:T(2,128)(2,1)S(1)} async-done(((bf16[1,2,1024,768]{3,1,0,2:T(2,128)(2,1)}), bf16[1,2,1024,768]{3,1,0,2:T(2,128)(2,1)S(1)}, u32[]{:S(2)}, u32[]{:S(2)}) %all-to-all-start.2) | async-done | bytes 3145760 | tf_op jit(solution)/shard_map/all_to_all | solution.py:71
  311.0 1.7 copy-done
  312.6 2.5 copy.50
  315.2 5.2 %gather_fusion.2 = bf16[1024,768]{1,0:T(8,128)(2,1)} fusion(bf16[2048,768]{1,0:T(8,128)(2,1)S(1)} %bitcast.64, s32[1024]{0:T(1024)S(1)} %broadcast_clamp_fusion.1), kind=kCustom, calls=%fused_computation.2 | custom fusion | bytes 3149824 | tf_op jit(solution)/shard_map/gather | solution.py:86
  320.4 4.2 %fusion.20 = (bf16[128,8,768]{2,1,0:T(8,128)(2,1)S(1)}, bf16[128,8,768]{2,1,0:T(8,128)(2,1)S(1)}, f32[128,8]{1,0:T(8,128)S(1)}) fusion(bf16[1024,768]{1,0:T(8,128)(2,1)} %gather_fusion.2, f32[128,8]{1,0:T(8,128)S(1)} %copy.43, bf16[128,8,1536]{2,1,0:T(8,128)(2,1)} %param.6, bf16[128,8,768]{2,1,0:T(8,128)(2,1)} %get-tuple-element.14), kind=kLoop, calls=%fused_computation.31 | loop fusion | flops 15727616 | bytes 9445376 | tf_op jit(solution)/shard_map/convert.2
  324.6 0.7 copy.54
  325.3 1.9 pad_maximum_fusion.1
  327.2 1.9 bitcast_convert_fusion
  (24 shorter events, 0.1 us)
Async XLA Ops:
  7.2 105.0 %all-gather.3.cloned.1.call-start = ((), (), s32[]{:S(2)}) async-start(), calls=%async_computation.4 | async-start | bytes 8912896 | tf_op jit(solution)/shard_map/all_gather | solution.py:26
  27.2 48.9 %copy-start.3 = (bf16[2,48,2048]{2,1,0:T(8,128)(2,1)S(1)}, bf16[2,48,2048]{2,1,0:T(8,128)(2,1)}, u32[]{:S(2)}) copy-start(bf16[2,48,2048]{2,1,0:T(8,128)(2,1)} %param.9) | copy-start | bytes 1179652
  79.6 160.5 %all-to-all-start.1 = ((bf16[16,2,48,2048]{3,2,1,0:T(8,128)(2,1)}), bf16[16,2,48,2048]{3,2,1,0:T(8,128)(2,1)}, u32[]{:S(2)}, u32[]{:S(2)}) async-start(bf16[16,2,48,2048]{3,2,1,0:T(8,128)(2,1)} %stack.4), calls=%async_computation.1 | async-start | bytes 12582912 | tf_op jit(solution)/shard_map/all_to_all | solution.py:29
  88.4 238.8 %reduce-scatter.2.cloned.1.call-start = ((), (), s32[]{:S(2)}) async-start(), calls=%async_computation.5 | async-start | bytes 6684672 | tf_op jit(solution)/shard_map/reduce_scatter | solution.py:84
  112.2 21.1 %copy-start.2 = (bf16[16,2,64,768]{3,2,0,1:T(8,128)(2,1)S(1)}, bf16[16,2,64,768]{3,2,0,1:T(8,128)(2,1)}, u32[]{:S(2)}) copy-start(bf16[16,2,64,768]{3,2,0,1:T(8,128)(2,1)} %copy.45) | copy-start | bytes 9437188
  133.3 6.0 %copy-start.1 = (bf16[2048,2048]{1,0:T(8,128)(2,1)S(1)}, bf16[2048,2048]{1,0:T(8,128)(2,1)}, u32[]{:S(2)}) copy-start(bf16[2048,2048]{1,0:T(8,128)(2,1)} %gather_fusion.1) | copy-start | bytes 25165828
  257.7 4.1 %copy-start.4 = (s32[128,8]{0,1:T(8,128)S(1)}, s32[128,8]{0,1:T(8,128)}, u32[]{:S(2)}) copy-start(s32[128,8]{0,1:T(8,128)} %param.7) | copy-start | bytes 12292
  257.7 53.2 %all-to-all-start.2 = ((bf16[1,2,1024,768]{3,1,0,2:T(2,128)(2,1)}), bf16[1,2,1024,768]{3,1,0,2:T(2,128)(2,1)S(1)}, u32[]{:S(2)}, u32[]{:S(2)}) async-start(bf16[1,2,1024,768]{3,1,0,2:T(2,128)(2,1)} %copy.49), calls=%async_computation.2 | async-start | bytes 6291456 | tf_op jit(solution)/shard_map/all_to_all | solution.py:71
  311.0 1.7 copy-start
Sparse Core Ops, SparseCore 0:
  10.4 100.7 all-gather.2
  146.5 123.6 reduce-scatter.1
